TPU v7x, 128 devices: a whole 4x4x4 slice. The times are simulated.
128 devices in a mesh: dp: 16 (over x, z_hi, core), ctx: 8 (over z_lo, y).
Axes of the slice: x: 4, y: 4, z: 4 (z_hi: 2, z_lo: 2; z = z_hi * 2 + z_lo), core: 2. Of those that a mesh axis runs over, the one named last changes fastest.
Arguments:
- light_flux: float32 [16, 6, 4096], P('dp', None, 'ctx'), may hold values from -6 to 6
- lengths: int32 [16], P('dp'), may hold values from 1024 to 4096, as said below
- offsets: int32 [16, 4096], P('dp', 'ctx'), may hold values from 0 to 3
- start_weight: float32 [512, 3], replicated, may hold values from -3.5 to 3.5
- conv_weight: bfloat16 [2, 1024, 1536], P(None, 'dp'), may hold values from -0.15625 to 0.15625
- gate_bias: float32 [2, 1024], replicated, may hold values from -4 to 4
- mix_first: bfloat16 [1024, 512], P('dp'), may hold values from -0.25 to 0.25
- mix_last: bfloat16 [512, 512], P('dp'), may hold values from -0.25 to 0.25
- end_weight: float32 [6, 512], replicated, may hold values from -0.25 to 0.25
- cotangent: float32 [16, 3, 4096], P('dp', None, 'ctx'), may hold values from -0.0234375 to 0.0234375
Outputs:
- coupled: float32 [16, 3, 4096], P('dp', None, 'ctx')
- grad_start: float32 [512, 3], replicated
- grad_conv: float32 [2, 1024, 1536], P(None, 'dp')
- grad_bias: float32 [2, 1024], replicated
- grad_mix_first: float32 [1024, 512], P('dp')
- grad_mix_last: float32 [512, 512], P('dp')
- grad_end: float32 [6, 512], replicated
Inputs may be any that keep to these rules, and one draw needn't show every extreme that they name: `lengths`: epochs at or past a curve's length are padding; at least one curve has no padding.
All inputs are finite; a program needn't handle non-finite values.
Results may differ from a plain program's by a relative error of at most 0.0091.
Values may be sent and summed in bfloat16 or wider, within the bound.
No kernel may reach another device: no remote copies, remote signals or barrier semaphores. Data moves between devices by JAX's collectives and lax.ppermute only.
A program may use at most 128 MiB of HBM per device.

v0:
```python
import jax
import jax.numpy as jnp
from jax import lax
from jax.sharding import PartitionSpec as P

BUCKETS = 4
highest = lax.Precision.HIGHEST


def from_behind(array, axis, by):
    size = lax.axis_size(axis)
    pairs = [(i, i + by) for i in range(size) if 0 <= i + by < size]
    return lax.ppermute(array, axis, pairs)


def tap_stack(padded, bucket, dilation, reach_len, col_count):
    centre = lax.slice_in_dim(padded, reach_len, reach_len + col_count, axis=1)
    left_tap = lax.slice_in_dim(
        padded, reach_len - dilation, reach_len - dilation + col_count, axis=1
    )
    right_tap = lax.slice_in_dim(
        padded, reach_len + dilation, reach_len + dilation + col_count, axis=1
    )
    for shift_k in range(1, BUCKETS):
        chosen = (bucket == shift_k)[None, :]
        left_start = reach_len - dilation - shift_k
        right_start = reach_len + dilation + shift_k
        left_tap = jnp.where(
            chosen, lax.slice_in_dim(padded, left_start, left_start + col_count, axis=1), left_tap
        )
        right_tap = jnp.where(
            chosen,
            lax.slice_in_dim(padded, right_start, right_start + col_count, axis=1),
            right_tap,
        )
    return jnp.concatenate([left_tap, centre, right_tap], axis=0)


def place_piece(piece, start_col, total_len):
    return jnp.pad(piece, ((0, 0), (start_col, total_len - start_col - piece.shape[1])))


def tap_transpose(d_stacked, bucket, dilation, reach_len, col_count, channels):
    total_len = col_count + 2 * reach_len
    d_left = d_stacked[:channels]
    d_centre = d_stacked[channels : 2 * channels]
    d_right = d_stacked[2 * channels :]
    window = place_piece(d_centre, reach_len, total_len)
    for shift_k in range(BUCKETS):
        chosen = (bucket == shift_k)[None, :]
        left_part = jnp.where(chosen, d_left, 0.0)
        right_part = jnp.where(chosen, d_right, 0.0)
        window = window + place_piece(left_part, reach_len - dilation - shift_k, total_len)
        window = window + place_piece(right_part, reach_len + dilation + shift_k, total_len)
    return window


def gate_forward(preact):
    channels = preact.shape[0] // 2
    return jnp.tanh(preact[:channels]) * jax.nn.sigmoid(preact[channels:])


def gate_backward(preact, d_gated):
    channels = preact.shape[0] // 2
    tangent = jnp.tanh(preact[:channels])
    sigmoid_part = jax.nn.sigmoid(preact[channels:])
    d_upper = d_gated * sigmoid_part * (1.0 - tangent * tangent)
    d_lower = d_gated * tangent * sigmoid_part * (1.0 - sigmoid_part)
    return jnp.concatenate([d_upper, d_lower], axis=0).astype(jnp.bfloat16)


def contract_rows(left_op, right_op, precision=None):
    return lax.dot_general(
        left_op,
        right_op,
        (((1,), (1,)), ((), ())),
        precision=precision,
        preferred_element_type=jnp.float32,
    )


def contract_cols(left_op, right_op, precision=None):
    return lax.dot_general(
        left_op,
        right_op,
        (((0,), (0,)), ((), ())),
        precision=precision,
        preferred_element_type=jnp.float32,
    )


def extend(hidden, reach_len, shard_len):
    pieces_low = []
    pieces_high = []
    remain = reach_len
    distance = 1
    while remain > 0:
        amount = min(shard_len, remain)
        from_low = from_behind(hidden[:, shard_len - amount :], "ctx", distance)
        from_high = from_behind(hidden[:, :amount], "ctx", -distance)
        pieces_low.insert(0, from_low)
        pieces_high.append(from_high)
        remain = remain - amount
        distance = distance + 1
    return jnp.concatenate(pieces_low + [hidden] + pieces_high, axis=1)


def return_rims(grad_window, reach_len, shard_len):
    middle = grad_window[:, reach_len : reach_len + shard_len]
    remain = reach_len
    distance = 1
    end_col = reach_len
    while remain > 0:
        amount = min(shard_len, remain)
        piece_low = grad_window[:, end_col - amount : end_col]
        high_start = reach_len + shard_len + (reach_len - remain)
        piece_high = grad_window[:, high_start : high_start + amount]
        back_low = from_behind(piece_low, "ctx", -distance)
        back_high = from_behind(piece_high, "ctx", distance)
        middle = middle + place_piece(back_low, shard_len - amount, shard_len)
        middle = middle + place_piece(back_high, 0, shard_len)
        end_col = end_col - amount
        remain = remain - amount
        distance = distance + 1
    return middle


def layer_forward(conv_shard, mix_shard, bias_row, stacked):
    full_conv, full_mix = (
        lax.all_gather(conv_shard, "dp", axis=0, tiled=True),
        lax.all_gather(mix_shard, "dp", axis=0, tiled=True),
    )
    preact = jnp.dot(full_conv, stacked, preferred_element_type=jnp.float32) + bias_row[:, None]
    gated = gate_forward(preact).astype(jnp.bfloat16)
    mixed_rows = jnp.dot(full_mix, gated, preferred_element_type=jnp.float32)
    return (preact, gated, mixed_rows, (full_conv, full_mix))


def mix_back(mix_weight, d_mixed):
    return contract_cols(mix_weight, d_mixed)


def conv_back(conv_weight_rows, dz_rows):
    return contract_cols(conv_weight_rows, dz_rows)


def reduce_grad(left_op, right_op):
    full_grad = contract_rows(left_op, right_op)
    summed = lax.psum(full_grad, "ctx")
    return lax.psum_scatter(summed, "dp", scatter_dimension=0, tiled=True)


def local(
    light_flux,
    lengths,
    offsets,
    start_weight,
    conv_weight,
    gate_bias,
    mix_first,
    mix_last,
    end_weight,
    cotangent,
):
    shard_len = light_flux.shape[2]
    half_bands = light_flux.shape[1] // 2
    channels = start_weight.shape[0]
    position = lax.axis_index("ctx") * shard_len + jnp.arange(shard_len, dtype=jnp.int32)
    valid_mask = (position < lengths[0]).astype(jnp.float32)
    bucket = offsets[0]
    first_half = light_flux[0, :half_bands]
    second_half = light_flux[0, half_bands:]
    dilations = (shard_len // 4, shard_len + shard_len // 2)
    reaches = (dilations[0] + BUCKETS - 1, dilations[1] + BUCKETS - 1)
    hidden_first = (jnp.dot(start_weight, first_half, precision=highest) * valid_mask).astype(
        jnp.bfloat16
    )
    stacked_first = tap_stack(
        extend(hidden_first, reaches[0], shard_len), bucket, dilations[0], reaches[0], shard_len
    )
    pre_first, gated_first, mixed_first, kept_first = layer_forward(
        conv_weight[0], mix_first, gate_bias[0], stacked_first
    )
    hidden_second = (
        (hidden_first.astype(jnp.float32) + mixed_first[:channels]) * valid_mask
    ).astype(jnp.bfloat16)
    stacked_second = tap_stack(
        extend(hidden_second, reaches[1], shard_len), bucket, dilations[1], reaches[1], shard_len
    )
    pre_second, gated_second, mixed_second, kept_second = layer_forward(
        conv_weight[1], mix_last, gate_bias[1], stacked_second
    )
    skip_total = mixed_first[channels:] + mixed_second
    end_out = jnp.dot(end_weight, skip_total, precision=highest)
    growth = jnp.exp(end_out[:half_bands])
    coupled = ((growth * second_half + end_out[half_bands:]) * valid_mask)[None]
    d_coupled = cotangent[0] * valid_mask
    d_end = jnp.concatenate([d_coupled * growth * second_half, d_coupled], axis=0)
    grad_end_local = contract_rows(d_end, skip_total, highest)
    d_skip = contract_cols(end_weight, d_end, highest)
    d_skip_b = d_skip.astype(jnp.bfloat16)
    d_gated_second = mix_back(kept_second[1], d_skip_b)
    grad_mix_last = reduce_grad(d_skip_b, gated_second)
    dz_second = gate_backward(pre_second, d_gated_second)
    grad_conv_second = reduce_grad(dz_second, stacked_second)
    bias_second = jnp.sum(dz_second.astype(jnp.float32), axis=1)
    d_stacked_second = conv_back(kept_second[0], dz_second)
    d_window_second = tap_transpose(
        d_stacked_second, bucket, dilations[1], reaches[1], shard_len, channels
    )
    d_field_second = return_rims(d_window_second, reaches[1], shard_len)
    d_mixed_first = jnp.concatenate([d_field_second * valid_mask, d_skip], axis=0).astype(
        jnp.bfloat16
    )
    d_gated_first = mix_back(kept_first[1], d_mixed_first)
    grad_mix_first = reduce_grad(d_mixed_first, gated_first)
    dz_first = gate_backward(pre_first, d_gated_first)
    grad_conv_first = reduce_grad(dz_first, stacked_first)
    bias_first = jnp.sum(dz_first.astype(jnp.float32), axis=1)
    d_stacked_first = conv_back(kept_first[0], dz_first)
    d_window_first = tap_transpose(
        d_stacked_first, bucket, dilations[0], reaches[0], shard_len, channels
    )
    d_hidden_first = d_field_second * valid_mask + return_rims(
        d_window_first, reaches[0], shard_len
    )
    grad_start_local = contract_rows(d_hidden_first * valid_mask, first_half, highest)
    grad_start, grad_bias, grad_end = lax.psum(
        (grad_start_local, jnp.stack([bias_first, bias_second]), grad_end_local), ("dp", "ctx")
    )
    grad_conv = jnp.stack([grad_conv_first, grad_conv_second])
    return (coupled, grad_start, grad_conv, grad_bias, grad_mix_first, grad_mix_last, grad_end)


def solution(mesh):
    in_specs = (
        P("dp", None, "ctx"),
        P("dp"),
        P("dp", "ctx"),
        P(),
        P(None, "dp", None),
        P(),
        P("dp", None),
        P("dp", None),
        P(),
        P("dp", None, "ctx"),
    )
    out_specs = (
        P("dp", None, "ctx"),
        P(),
        P(None, "dp", None),
        P(),
        P("dp", None),
        P("dp", None),
        P(),
    )
    return jax.shard_map(local, mesh=mesh, in_specs=in_specs, out_specs=out_specs, check_vma=False)
```

profile of v0, /device:TPU:1, one launch (start us, length us, event | category | flops | bytes accessed | tf_op | source)
XLA Modules:
  0.0 635.6 jit_solution(13438480193903545730)
XLA Ops:
  7.3 1.8 fusion.83
  13.8 4.0 collective-permute-start
  20.1 3.8 collective-permute-done.1
  23.9 4.0 fusion.43
  28.0 39.5 %all-gather.8.cloned.1.call-done = bf16[1,1024,1536]{2,1,0:T(8,128)(2,1)} async-done(((bf16[1,64,1536]{2,1,0:T(8,128)(2,1)}), bf16[1,1024,1536]{2,1,0:T(8,128)(2,1)}) %all-gather.8.cloned.1.call-update) | async-done | bytes 3145744 | tf_op jit(solution)/shard_map/all_gather | solution.py:130
  67.5 3.7 add_bitcast_fusion.1
  73.0 40.6 %all-gather.6.cloned.1.call-done = bf16[1024,512]{1,0:T(8,128)(2,1)} async-done(((bf16[64,512]{1,0:T(8,128)(2,1)}), bf16[1024,512]{1,0:T(8,128)(2,1)}) %all-gather.6.cloned.1.call-update) | async-done | bytes 1048592 | tf_op jit(solution)/shard_map/all_gather | solution.py:131
  113.6 2.0 convolution_bitcast_fusion.2
  117.1 4.0 collective-permute-start.3
  121.2 4.6 collective-permute-start.2
  127.1 36.2 %all_gather.15 = bf16[512,512]{1,0:T(8,128)(2,1)} all-gather(bf16[32,512]{1,0:T(8,128)(2,1)S(1)} %copy-done.31), channel_id=1, replica_groups=mesh['dp'=16,'ctx'=8] {'dp'}, dimensions={0}, use_global_device_ids=true | all-gather | bytes 557056 | tf_op jit(solution)/shard_map/all_gather | solution.py:131
  163.4 2.8 fusion.49
  166.2 13.4 %all-gather.10.cloned.1.call-done = bf16[1,1024,1536]{2,1,0:T(8,128)(2,1)} async-done(((bf16[1,64,1536]{2,1,0:T(8,128)(2,1)}), bf16[1,1024,1536]{2,1,0:T(8,128)(2,1)}) %all-gather.10.cloned.1.call-update) | async-done | bytes 3145744 | tf_op jit(solution)/shard_map/all_gather | solution.py:130
  179.6 3.9 add_bitcast_fusion
  189.3 1.8 convolution_bitcast_fusion.1
  193.4 2.0 copy-done.2
  198.2 5.0 collective-permute-start.7
  207.4 5.7 collective-permute-start.9
  213.1 26.5 %collective-permute-done.8 = f32[512,259]{0,1:T(8,128)S(1)} collective-permute-done((f32[512,259]{0,1:T(8,128)S(1)}, f32[512,259]{0,1:T(8,128)S(1)}, u32[]{:S(2)}, u32[]{:S(2)}) %collective-permute-start.8) | collective-permute-done | bytes 530464 | tf_op jit(solution)/shard_map/ppermute | solution.py:13
  239.5 2.9 fusion.76
  243.2 2.1 fusion.31
  245.4 5.7 fusion.32
  252.4 2.8 multiply_convert_fusion.1
  256.2 4.5 fusion.33
  261.9 3.7 convolution_bitcast_fusion
  267.7 10.9 %reduce-scatter.11.cloned.1.call-done = f32[32,512]{1,0:T(8,128)} async-done(((f32[512,512]{1,0:T(8,128)}), f32[32,512]{1,0:T(8,128)}) %reduce-scatter.11.cloned.1.call-update) | async-done | bytes 65552 | tf_op jit(solution)/shard_map/reduce_scatter | solution.py:150
  278.6 74.3 %reduce-scatter.9.cloned.1.call-done = f32[64,512]{1,0:T(8,128)} async-done(((f32[1024,512]{1,0:T(8,128)}), f32[64,512]{1,0:T(8,128)}) %reduce-scatter.9.cloned.1.call-update) | async-done | bytes 131088 | tf_op jit(solution)/shard_map/reduce_scatter | solution.py:150
  352.9 93.9 %reduce-scatter.7.cloned.1.call-done = f32[64,1536]{1,0:T(8,128)} async-done(((f32[1024,1536]{1,0:T(8,128)}), f32[64,1536]{1,0:T(8,128)}) %reduce-scatter.7.cloned.1.call-update) | async-done | bytes 393232 | tf_op jit(solution)/shard_map/reduce_scatter | solution.py:150
  446.8 93.0 %reduce-scatter.5.cloned.1.call-done = f32[64,1536]{1,0:T(8,128)} async-done(((f32[1024,1536]{1,0:T(8,128)}), f32[64,1536]{1,0:T(8,128)}) %reduce-scatter.5.cloned.1.call-update) | async-done | bytes 393232 | tf_op jit(solution)/shard_map/reduce_scatter | solution.py:150
  541.3 4.0 collective-permute-start.11
  549.9 73.7 %all-reduce.22 = (f32[512,3]{0,1:T(4,128)}, f32[2,1024]{1,0:T(2,128)}, f32[6,512]{1,0:T(8,128)}) all-reduce(f32[512,3]{0,1:T(4,128)S(1)} %fusion.15, f32[2,1024]{1,0:T(2,128)S(1)} %pad_maximum_fusion.22, f32[6,512]{1,0:T(8,128)S(1)} %fusion.55), channel_id=1, replica_groups=mesh['dp'=16,'ctx'=8] {'dp','ctx'}, use_global_device_ids=true, to_apply=%region_0.1 | all-reduce | flops 6656 | bytes 53248 | tf_op jit(solution)/shard_map/psum | solution.py:228
  623.7 2.1 pad_maximum_fusion.5
  (137 shorter events, 41.4 us)
Async XLA Ops:
  7.2 177.9 %copy-start = (f32[6,512]{1,0:T(8,128)S(1)}, f32[6,512]{1,0:T(8,128)}, u32[]{:S(2)}) copy-start(f32[6,512]{1,0:T(8,128)} %param.18) | copy-start | bytes 36868
  7.2 11.9 %copy-start.32 = (f32[2,1024]{1,0:T(2,128)S(1)}, f32[2,1024]{1,0:T(2,128)}, u32[]{:S(2)}) copy-start(f32[2,1024]{1,0:T(2,128)} %param.15) | copy-start | bytes 24580
  7.2 11.9 %copy-start.34 = (s32[1,512]{1,0:T(1,128)S(1)}, s32[1,512]{1,0:T(1,128)}, u32[]{:S(2)}) copy-start(s32[1,512]{1,0:T(1,128)} %param.12) | copy-start | bytes 6148
  7.2 60.3 %all-gather.8.cloned.1.call-start = ((), (), s32[]{:S(2)}) async-start(), calls=%async_computation.5 | async-start | bytes 3342336 | tf_op jit(solution)/shard_map/all_gather | solution.py:130
  9.1 104.5 %all-gather.6.cloned.1.call-start = ((), (), s32[]{:S(2)}) async-start(), calls=%async_computation.4 | async-start | bytes 1114112 | tf_op jit(solution)/shard_map/all_gather | solution.py:131
  9.8 169.8 %all-gather.10.cloned.1.call-start = ((), (), s32[]{:S(2)}) async-start(), calls=%async_computation.6 | async-start | bytes 3342336 | tf_op jit(solution)/shard_map/all_gather | solution.py:130
  10.6 268.1 %reduce-scatter.11.cloned.1.call-start = ((), (), s32[]{:S(2)}) async-start(), calls=%async_computation.10 | async-start | bytes 1114112 | tf_op jit(solution)/shard_map/reduce_scatter | solution.py:150
  13.7 101.8 %copy-start.3 = (bf16[512,512]{0,1:T(8,128)(2,1)}, bf16[512,512]{0,1:T(8,128)(2,1)S(1)}, u32[]{:S(2)}) copy-start(bf16[512,512]{0,1:T(8,128)(2,1)S(1)} %fusion.11) | copy-start | bytes 1572868
  13.8 6.4 collective-permute-start
  17.8 6.1 collective-permute-start.1
  27.9 39.5 %copy-start.26 = (bf16[512,512]{0,1:T(8,128)(2,1)}, bf16[512,512]{0,1:T(8,128)(2,1)S(1)}, u32[]{:S(2)}) copy-start(bf16[512,512]{0,1:T(8,128)(2,1)S(1)} %get-tuple-element.69) | copy-start | bytes 1572868
  28.0 43.2 %copy-start.28 = (bf16[512,512]{0,1:T(8,128)(2,1)}, bf16[512,512]{0,1:T(8,128)(2,1)S(1)}, u32[]{:S(2)}) copy-start(bf16[512,512]{0,1:T(8,128)(2,1)S(1)} %get-tuple-element.70) | copy-start | bytes 1572868
  73.0 40.6 %copy-start.8 = (bf16[512,512]{0,1:T(8,128)(2,1)}, bf16[512,512]{0,1:T(8,128)(2,1)S(1)}, u32[]{:S(2)}) copy-start(bf16[512,512]{0,1:T(8,128)(2,1)S(1)} %multiply_convert_fusion.5) | copy-start | bytes 1572868
  115.8 63.9 %copy-start.6 = (bf16[512,512]{0,1:T(8,128)(2,1)}, bf16[512,512]{0,1:T(8,128)(2,1)S(1)}, u32[]{:S(2)}) copy-start(bf16[512,512]{0,1:T(8,128)(2,1)S(1)} %fusion.25) | copy-start | bytes 1572868
  115.8 47.5 %collective-permute-start.4 = (bf16[512,512]{0,1:T(8,128)(2,1)S(1)}, bf16[512,512]{0,1:T(8,128)(2,1)S(1)}, u32[]{:S(2)}, u32[]{:S(2)}) collective-permute-start(bf16[512,512]{0,1:T(8,128)(2,1)S(1)} %fusion.25), channel_id=1, source_target_pairs={{1,0},{2,1},{3,2},{4,3},{5,4},{6,5},{7,6},{9,8},{10,9},{11,10},{12... | collective-permute-start | bytes 1572872 | tf_op jit(solution)/shard_map/ppermute | solution.py:13
  117.1 46.3 %collective-permute-start.3 = (bf16[512,512]{0,1:T(8,128)(2,1)S(1)}, bf16[512,512]{0,1:T(8,128)(2,1)S(1)}, u32[]{:S(2)}, u32[]{:S(2)}) collective-permute-start(bf16[512,512]{0,1:T(8,128)(2,1)S(1)} %fusion.25), channel_id=1, source_target_pairs={{0,1},{1,2},{2,3},{3,4},{4,5},{5,6},{6,7},{8,9},{9,10},{10,11},{11... | collective-permute-start | bytes 1572872 | tf_op jit(solution)/shard_map/ppermute | solution.py:13
  121.2 42.2 %collective-permute-start.2 = (bf16[512,259]{0,1:T(8,128)(2,1)S(1)}, bf16[512,259]{0,1:T(8,128)(2,1)S(1)}, u32[]{:S(2)}, u32[]{:S(2)}) collective-permute-start(bf16[512,259]{0,1:T(8,128)(2,1)S(1)} %get-tuple-element.71), channel_id=1, source_target_pairs={{0,2},{1,3},{2,4},{3,5},{4,6},{5,7},{8,10},{9,11},{10,12},{11,13},... | collective-permute-start | bytes 795656 | tf_op jit(solution)/shard_map/ppermute | solution.py:13
  125.8 37.6 %collective-permute-start.5 = (bf16[512,259]{0,1:T(8,128)(2,1)S(1)}, bf16[512,259]{0,1:T(8,128)(2,1)S(1)}, u32[]{:S(2)}, u32[]{:S(2)}) collective-permute-start(bf16[512,259]{0,1:T(8,128)(2,1)S(1)} %get-tuple-element.72), channel_id=1, source_target_pairs={{2,0},{3,1},{4,2},{5,3},{6,4},{7,5},{10,8},{11,9},{12,10},{13,11},... | collective-permute-start | bytes 795656 | tf_op jit(solution)/shard_map/ppermute | solution.py:13
  166.2 17.3 %copy-start.13 = (bf16[512,512]{0,1:T(8,128)(2,1)}, bf16[512,512]{0,1:T(8,128)(2,1)S(1)}, u32[]{:S(2)}) copy-start(bf16[512,512]{0,1:T(8,128)(2,1)S(1)} %get-tuple-element.84) | copy-start | bytes 1572868
  197.0 42.6 %collective-permute-start.6 = (f32[512,512]{0,1:T(8,128)}, f32[512,512]{0,1:T(8,128)S(1)}, u32[]{:S(2)}, u32[]{:S(2)}) collective-permute-start(f32[512,512]{0,1:T(8,128)} %get-tuple-element.27), channel_id=1, source_target_pairs={{1,0},{2,1},{3,2},{4,3},{5,4},{6,5},{7,6},{9,8},{10,9},{11,10},{12... | collective-permute-start | bytes 3145736 | tf_op jit(solution)/shard_map/ppermute | solution.py:13
  198.2 41.3 %collective-permute-start.7 = (f32[512,512]{0,1:T(8,128)}, f32[512,512]{0,1:T(8,128)}, u32[]{:S(2)}, u32[]{:S(2)}) collective-permute-start(f32[512,512]{0,1:T(8,128)} %get-tuple-element.28), channel_id=1, source_target_pairs={{0,1},{1,2},{2,3},{3,4},{4,5},{5,6},{6,7},{8,9},{9,10},{10,11},{11... | collective-permute-start | bytes 3145736 | tf_op jit(solution)/shard_map/ppermute | solution.py:13
  204.7 148.2 %reduce-scatter.9.cloned.1.call-start = ((), (), s32[]{:S(2)}) async-start(), calls=%async_computation.9 | async-start | bytes 2228224 | tf_op jit(solution)/shard_map/reduce_scatter | solution.py:150
  206.1 33.4 %collective-permute-start.8 = (f32[512,259]{0,1:T(8,128)S(1)}, f32[512,259]{0,1:T(8,128)S(1)}, u32[]{:S(2)}, u32[]{:S(2)}) collective-permute-start(f32[512,259]{0,1:T(8,128)S(1)} %get-tuple-element.29), channel_id=1, source_target_pairs={{2,0},{3,1},{4,2},{5,3},{6,4},{7,5},{10,8},{11,9},{12,10},{13,11},... | collective-permute-start | bytes 1591304 | tf_op jit(solution)/shard_map/ppermute | solution.py:13
  207.4 35.8 %copy-start.9 = (bf16[512,512]{0,1:T(8,128)(2,1)S(1)}, bf16[512,512]{0,1:T(8,128)(2,1)}, u32[]{:S(2)}) copy-start(bf16[512,512]{0,1:T(8,128)(2,1)} %copy-done.8) | copy-start | bytes 1572868
  207.4 32.1 %collective-permute-start.9 = (f32[512,259]{0,1:T(8,128)S(1)}, f32[512,259]{0,1:T(8,128)S(1)}, u32[]{:S(2)}, u32[]{:S(2)}) collective-permute-start(f32[512,259]{0,1:T(8,128)S(1)} %get-tuple-element.30), channel_id=1, source_target_pairs={{0,2},{1,3},{2,4},{3,5},{4,6},{5,7},{8,10},{9,11},{10,12},{11,13},... | collective-permute-start | bytes 1591304 | tf_op jit(solution)/shard_map/ppermute | solution.py:13
  245.3 201.5 %reduce-scatter.7.cloned.1.call-start = ((), (), s32[]{:S(2)}) async-start(), calls=%async_computation.8 | async-start | bytes 6684672 | tf_op jit(solution)/shard_map/reduce_scatter | solution.py:150
  251.2 288.6 %reduce-scatter.5.cloned.1.call-start = ((), (), s32[]{:S(2)}) async-start(), calls=%async_computation.7 | async-start | bytes 6684672 | tf_op jit(solution)/shard_map/reduce_scatter | solution.py:150
  260.8 362.9 %all-reduce.26.cloned.1.call-start = ((), (), s32[]{:S(2)}) async-start(), calls=%async_computation.11 | async-start | bytes 1966080 | tf_op jit(solution)/shard_map/psum | solution.py:149
  267.7 278.9 %copy-start.17 = (bf16[512,512]{0,1:T(8,128)(2,1)S(1)}, bf16[512,512]{0,1:T(8,128)(2,1)}, u32[]{:S(2)}) copy-start(bf16[512,512]{0,1:T(8,128)(2,1)} %copy-done.16) | copy-start | bytes 1572868
  539.9 8.3 %collective-permute-start.10 = (f32[512,131]{0,1:T(8,128)S(1)}, f32[512,131]{0,1:T(8,128)S(1)}, u32[]{:S(2)}, u32[]{:S(2)}) collective-permute-start(f32[512,131]{0,1:T(8,128)S(1)} %get-tuple-element.67), channel_id=1, source_target_pairs={{1,0},{2,1},{3,2},{4,3},{5,4},{6,5},{7,6},{9,8},{10,9},{11,10},{12... | collective-permute-start | bytes 804872 | tf_op jit(solution)/shard_map/ppermute | solution.py:13
  541.3 7.7 %collective-permute-start.11 = (f32[512,131]{0,1:T(8,128)S(1)}, f32[512,131]{0,1:T(8,128)S(1)}, u32[]{:S(2)}, u32[]{:S(2)}) collective-permute-start(f32[512,131]{0,1:T(8,128)S(1)} %get-tuple-element.68), channel_id=1, source_target_pairs={{0,1},{1,2},{2,3},{3,4},{4,5},{5,6},{6,7},{8,9},{9,10},{10,11},{11... | collective-permute-start | bytes 804872 | tf_op jit(solution)/shard_map/ppermute | solution.py:13
  549.1 79.7 %copy-start.1 = (f32[6,512]{1,0:T(8,128)S(1)}, f32[6,512]{1,0:T(8,128)}, u32[]{:S(2)}) copy-start(f32[6,512]{1,0:T(8,128)} %param.18) | copy-start | bytes 36868
  (24 other events, 80.9 us)
Sparse Core Ops, SparseCore 0:
  11.0 56.4 all-gather.7
  69.9 43.6 all-gather.5
  116.0 63.5 all-gather.9
  204.8 73.7 reduce-scatter.10
  282.9 69.9 reduce-scatter.8
  357.5 89.2 reduce-scatter.6
  451.5 88.2 reduce-scatter.4
  542.8 71.9 all-reduce.25
where the time goes:
time: 637 us; the launch traced here: 636 us
  waiting for transfers between devices  400 us (63%)
  blocking collectives  110 us (17%)
  matrix products  38.1 us (6%)
  starting transfers between devices  35.7 us (6%)
  local copies, waits for them, and re-layouts  18.5 us (3%)
  other arithmetic  17.6 us (3%)
  between operations  15.4 us (2%)
    reduce_scatter x4, waiting for transfers between devices, reduce_grad(): return lax.psum_scatter(summed, 'dp', scatter_dimension=0, tiled=True)  272 us
    psum x1, blocking collectives, local(): lax.psum((grad_start_local, jnp.stack([bias_first, bias_second]), grad_en...  73.7 us
    all_gather x2, waiting for transfers between devices, layer_forward(): lax.all_gather(conv_shard, 'dp', axis=0, tiled=True)  52.9 us
    all_gather x1, waiting for transfers between devices, layer_forward(): lax.all_gather(mix_shard, 'dp', axis=0, tiled=True)  40.6 us
    all_gather x1, blocking collectives, layer_forward(): lax.all_gather(mix_shard, 'dp', axis=0, tiled=True)  36.2 us
    ppermute x12, starting transfers between devices, from_behind(): return lax.ppermute(array, axis, pairs)  35.2 us
    ppermute x12, waiting for transfers between devices, from_behind(): return lax.ppermute(array, axis, pairs)  33.3 us
    dot_general x6, matrix products, contract_rows(): lax.dot_general(left_op, right_op, (((1,), (1,)), ((), ())), precision=pr...  15.2 us
  transfers between devices with their start and end apart: 20, of which 12 were waited for; matrix products, arithmetic and copies ran while one was open for 7% of the time, Pallas kernels for 0%

commit v1 on v0

--- a/solution.py
+++ b/solution.py
@@ -226,7 +226,8 @@
     )
     grad_start_local = contract_rows(d_hidden_first * valid_mask, first_half, highest)
     grad_start, grad_bias, grad_end = lax.psum(
-        (grad_start_local, jnp.stack([bias_first, bias_second]), grad_end_local), ("dp", "ctx")
+        lax.psum((grad_start_local, jnp.stack([bias_first, bias_second]), grad_end_local), "ctx"),
+        "dp",
     )
     grad_conv = jnp.stack([grad_conv_first, grad_conv_second])
     return (coupled, grad_start, grad_conv, grad_bias, grad_mix_first, grad_mix_last, grad_end)

time: 637 us -> 668 us (1.049)
  blocking collectives: 110 us -> 135 us
    psum x0 -> x1, blocking collectives: none -> 70.1 us  [local(): lax.psum(lax.psum((grad_start_local, jnp.stack([bias_first, bias_second])...]
    psum x1, blocking collectives: 73.7 us -> 28.6 us  [local(): lax.psum((grad_start_local, jnp.stack([bias_first, bias_second]), grad_en...]
where the time goes in v1:
time: 668 us; the launch traced here: 660 us
  waiting for transfers between devices  400 us (60%)
  blocking collectives  135 us (20%)
  matrix products  38.1 us (6%)
  starting transfers between devices  35.7 us (5%)
  local copies, waits for them, and re-layouts  18.5 us (3%)
  other arithmetic  17.6 us (3%)
  between operations  15.4 us (2%)
    reduce_scatter x4, waiting for transfers between devices, reduce_grad(): return lax.psum_scatter(summed, 'dp', scatter_dimension=0, tiled=True)  272 us
    psum x1, blocking collectives, local(): lax.psum(lax.psum((grad_start_local, jnp.stack([bias_first, bias_second])...  70.1 us
    all_gather x2, waiting for transfers between devices, layer_forward(): lax.all_gather(conv_shard, 'dp', axis=0, tiled=True)  52.9 us
    all_gather x1, waiting for transfers between devices, layer_forward(): lax.all_gather(mix_shard, 'dp', axis=0, tiled=True)  40.5 us
    all_gather x1, blocking collectives, layer_forward(): lax.all_gather(mix_shard, 'dp', axis=0, tiled=True)  36.2 us
    ppermute x12, starting transfers between devices, from_behind(): return lax.ppermute(array, axis, pairs)  35.2 us
    ppermute x12, waiting for transfers between devices, from_behind(): return lax.ppermute(array, axis, pairs)  33.1 us
    psum x1, blocking collectives, local(): lax.psum((grad_start_local, jnp.stack([bias_first, bias_second]), grad_en...  28.6 us
  transfers between devices with their start and end apart: 20, of which 12 were waited for; matrix products, arithmetic and copies ran while one was open for 7% of the time, Pallas kernels for 0%

profile of v1, /device:TPU:1, one launch (start us, length us, event | category | flops | bytes accessed | tf_op | source)
XLA Modules:
  0.0 660.1 jit_solution(1660582100547987181)
XLA Ops:
  13.7 4.0 collective-permute-start
  20.1 3.8 collective-permute-done.1
  23.9 4.0 fusion.43
  28.0 39.5 %all-gather.8.cloned.1.call-done = bf16[1,1024,1536]{2,1,0:T(8,128)(2,1)} async-done(((bf16[1,64,1536]{2,1,0:T(8,128)(2,1)}), bf16[1,1024,1536]{2,1,0:T(8,128)(2,1)}) %all-gather.8.cloned.1.call-update) | async-done | bytes 3145744 | tf_op jit(solution)/shard_map/all_gather | solution.py:130
  67.5 3.7 add_bitcast_fusion.1
  73.0 40.5 %all-gather.6.cloned.1.call-done = bf16[1024,512]{1,0:T(8,128)(2,1)} async-done(((bf16[64,512]{1,0:T(8,128)(2,1)}), bf16[1024,512]{1,0:T(8,128)(2,1)}) %all-gather.6.cloned.1.call-update) | async-done | bytes 1048592 | tf_op jit(solution)/shard_map/all_gather | solution.py:131
  113.6 2.0 convolution_bitcast_fusion.2
  117.1 4.0 collective-permute-start.3
  121.2 4.6 collective-permute-start.2
  127.1 36.2 %all_gather.15 = bf16[512,512]{1,0:T(8,128)(2,1)} all-gather(bf16[32,512]{1,0:T(8,128)(2,1)S(1)} %copy-done.31), channel_id=1, replica_groups=mesh['dp'=16,'ctx'=8] {'dp'}, dimensions={0}, use_global_device_ids=true | all-gather | bytes 557056 | tf_op jit(solution)/shard_map/all_gather | solution.py:131
  163.4 2.8 fusion.49
  166.2 13.4 %all-gather.10.cloned.1.call-done = bf16[1,1024,1536]{2,1,0:T(8,128)(2,1)} async-done(((bf16[1,64,1536]{2,1,0:T(8,128)(2,1)}), bf16[1,1024,1536]{2,1,0:T(8,128)(2,1)}) %all-gather.10.cloned.1.call-update) | async-done | bytes 3145744 | tf_op jit(solution)/shard_map/all_gather | solution.py:130
  179.6 3.9 add_bitcast_fusion
  189.3 1.8 convolution_bitcast_fusion.1
  193.4 2.0 copy-done.2
  198.2 5.0 collective-permute-start.7
  207.3 5.7 collective-permute-start.9
  213.0 26.5 %collective-permute-done.8 = f32[512,259]{0,1:T(8,128)S(1)} collective-permute-done((f32[512,259]{0,1:T(8,128)S(1)}, f32[512,259]{0,1:T(8,128)S(1)}, u32[]{:S(2)}, u32[]{:S(2)}) %collective-permute-start.8) | collective-permute-done | bytes 530464 | tf_op jit(solution)/shard_map/ppermute | solution.py:13
  239.5 2.9 fusion.76
  243.2 2.1 fusion.31
  245.4 5.7 fusion.32
  252.3 2.8 multiply_convert_fusion.1
  256.2 4.5 fusion.33
  261.9 3.7 convolution_bitcast_fusion
  267.7 10.9 %reduce-scatter.11.cloned.1.call-done = f32[32,512]{1,0:T(8,128)} async-done(((f32[512,512]{1,0:T(8,128)}), f32[32,512]{1,0:T(8,128)}) %reduce-scatter.11.cloned.1.call-update) | async-done | bytes 65552 | tf_op jit(solution)/shard_map/reduce_scatter | solution.py:150
  278.6 74.3 %reduce-scatter.9.cloned.1.call-done = f32[64,512]{1,0:T(8,128)} async-done(((f32[1024,512]{1,0:T(8,128)}), f32[64,512]{1,0:T(8,128)}) %reduce-scatter.9.cloned.1.call-update) | async-done | bytes 131088 | tf_op jit(solution)/shard_map/reduce_scatter | solution.py:150
  352.9 93.8 %reduce-scatter.7.cloned.1.call-done = f32[64,1536]{1,0:T(8,128)} async-done(((f32[1024,1536]{1,0:T(8,128)}), f32[64,1536]{1,0:T(8,128)}) %reduce-scatter.7.cloned.1.call-update) | async-done | bytes 393232 | tf_op jit(solution)/shard_map/reduce_scatter | solution.py:150
  446.7 92.9 %reduce-scatter.5.cloned.1.call-done = f32[64,1536]{1,0:T(8,128)} async-done(((f32[1024,1536]{1,0:T(8,128)}), f32[64,1536]{1,0:T(8,128)}) %reduce-scatter.5.cloned.1.call-update) | async-done | bytes 393232 | tf_op jit(solution)/shard_map/reduce_scatter | solution.py:150
  541.2 4.0 collective-permute-start.11
  549.5 28.6 %all-reduce.23 = (f32[512,3]{0,1:T(4,128)S(1)}, f32[2,1024]{1,0:T(2,128)S(1)}, f32[6,512]{1,0:T(8,128)S(1)}) all-reduce(f32[512,3]{0,1:T(4,128)S(1)} %fusion.15, f32[2,1024]{1,0:T(2,128)S(1)} %pad_maximum_fusion.22, f32[6,512]{1,0:T(8,128)S(1)} %fusion.55), channel_id=1, replica_groups=mesh['dp'=16,'ctx'=8] {'ctx'}, use_global_device_ids=true, to_apply=%region_0.1 | all-reduce | flops 6656 | bytes 53248 | tf_op jit(solution)/shard_map/psum | solution.py:229
  578.1 70.1 %all-reduce.22 = (f32[512,3]{0,1:T(4,128)}, f32[2,1024]{1,0:T(2,128)}, f32[6,512]{1,0:T(8,128)}) all-reduce(f32[512,3]{0,1:T(4,128)S(1)} %get-tuple-element.21, f32[2,1024]{1,0:T(2,128)S(1)} %get-tuple-element.22, f32[6,512]{1,0:T(8,128)S(1)} %get-tuple-element.23), channel_id=1, replica_groups=mesh['dp'=16,'ctx'=8] {'dp'}, use_global_device_ids=true, to_apply=%region_1.2 | all-reduce | flops 6656 | bytes 53248 | tf_op jit(solution)/shard_map/psum | solution.py:228
  648.2 2.1 pad_maximum_fusion.5
  (138 shorter events, 42.9 us)
Async XLA Ops:
  7.2 177.9 %copy-start = (f32[6,512]{1,0:T(8,128)S(1)}, f32[6,512]{1,0:T(8,128)}, u32[]{:S(2)}) copy-start(f32[6,512]{1,0:T(8,128)} %param.18) | copy-start | bytes 36868
  7.2 11.9 %copy-start.32 = (f32[2,1024]{1,0:T(2,128)S(1)}, f32[2,1024]{1,0:T(2,128)}, u32[]{:S(2)}) copy-start(f32[2,1024]{1,0:T(2,128)} %param.15) | copy-start | bytes 24580
  7.2 11.9 %copy-start.34 = (s32[1,512]{1,0:T(1,128)S(1)}, s32[1,512]{1,0:T(1,128)}, u32[]{:S(2)}) copy-start(s32[1,512]{1,0:T(1,128)} %param.12) | copy-start | bytes 6148
  7.2 60.3 %all-gather.8.cloned.1.call-start = ((), (), s32[]{:S(2)}) async-start(), calls=%async_computation.5 | async-start | bytes 3342336 | tf_op jit(solution)/shard_map/all_gather | solution.py:130
  9.1 104.5 %all-gather.6.cloned.1.call-start = ((), (), s32[]{:S(2)}) async-start(), calls=%async_computation.4 | async-start | bytes 1114112 | tf_op jit(solution)/shard_map/all_gather | solution.py:131
  9.8 169.8 %all-gather.10.cloned.1.call-start = ((), (), s32[]{:S(2)}) async-start(), calls=%async_computation.6 | async-start | bytes 3342336 | tf_op jit(solution)/shard_map/all_gather | solution.py:130
  10.5 268.1 %reduce-scatter.11.cloned.1.call-start = ((), (), s32[]{:S(2)}) async-start(), calls=%async_computation.10 | async-start | bytes 1114112 | tf_op jit(solution)/shard_map/reduce_scatter | solution.py:150
  13.7 101.8 %copy-start.3 = (bf16[512,512]{0,1:T(8,128)(2,1)}, bf16[512,512]{0,1:T(8,128)(2,1)S(1)}, u32[]{:S(2)}) copy-start(bf16[512,512]{0,1:T(8,128)(2,1)S(1)} %fusion.11) | copy-start | bytes 1572868
  13.7 6.4 collective-permute-start
  17.8 6.1 collective-permute-start.1
  27.9 39.5 %copy-start.26 = (bf16[512,512]{0,1:T(8,128)(2,1)}, bf16[512,512]{0,1:T(8,128)(2,1)S(1)}, u32[]{:S(2)}) copy-start(bf16[512,512]{0,1:T(8,128)(2,1)S(1)} %get-tuple-element.72) | copy-start | bytes 1572868
  27.9 43.2 %copy-start.28 = (bf16[512,512]{0,1:T(8,128)(2,1)}, bf16[512,512]{0,1:T(8,128)(2,1)S(1)}, u32[]{:S(2)}) copy-start(bf16[512,512]{0,1:T(8,128)(2,1)S(1)} %get-tuple-element.73) | copy-start | bytes 1572868
  73.0 40.6 %copy-start.8 = (bf16[512,512]{0,1:T(8,128)(2,1)}, bf16[512,512]{0,1:T(8,128)(2,1)S(1)}, u32[]{:S(2)}) copy-start(bf16[512,512]{0,1:T(8,128)(2,1)S(1)} %multiply_convert_fusion.5) | copy-start | bytes 1572868
  115.7 63.9 %copy-start.6 = (bf16[512,512]{0,1:T(8,128)(2,1)}, bf16[512,512]{0,1:T(8,128)(2,1)S(1)}, u32[]{:S(2)}) copy-start(bf16[512,512]{0,1:T(8,128)(2,1)S(1)} %fusion.25) | copy-start | bytes 1572868
  115.8 47.5 %collective-permute-start.4 = (bf16[512,512]{0,1:T(8,128)(2,1)S(1)}, bf16[512,512]{0,1:T(8,128)(2,1)S(1)}, u32[]{:S(2)}, u32[]{:S(2)}) collective-permute-start(bf16[512,512]{0,1:T(8,128)(2,1)S(1)} %fusion.25), channel_id=1, source_target_pairs={{1,0},{2,1},{3,2},{4,3},{5,4},{6,5},{7,6},{9,8},{10,9},{11,10},{12... | collective-permute-start | bytes 1572872 | tf_op jit(solution)/shard_map/ppermute | solution.py:13
  117.1 46.3 %collective-permute-start.3 = (bf16[512,512]{0,1:T(8,128)(2,1)S(1)}, bf16[512,512]{0,1:T(8,128)(2,1)S(1)}, u32[]{:S(2)}, u32[]{:S(2)}) collective-permute-start(bf16[512,512]{0,1:T(8,128)(2,1)S(1)} %fusion.25), channel_id=1, source_target_pairs={{0,1},{1,2},{2,3},{3,4},{4,5},{5,6},{6,7},{8,9},{9,10},{10,11},{11... | collective-permute-start | bytes 1572872 | tf_op jit(solution)/shard_map/ppermute | solution.py:13
  121.2 42.2 %collective-permute-start.2 = (bf16[512,259]{0,1:T(8,128)(2,1)S(1)}, bf16[512,259]{0,1:T(8,128)(2,1)S(1)}, u32[]{:S(2)}, u32[]{:S(2)}) collective-permute-start(bf16[512,259]{0,1:T(8,128)(2,1)S(1)} %get-tuple-element.74), channel_id=1, source_target_pairs={{0,2},{1,3},{2,4},{3,5},{4,6},{5,7},{8,10},{9,11},{10,12},{11,13},... | collective-permute-start | bytes 795656 | tf_op jit(solution)/shard_map/ppermute | solution.py:13
  125.8 37.6 %collective-permute-start.5 = (bf16[512,259]{0,1:T(8,128)(2,1)S(1)}, bf16[512,259]{0,1:T(8,128)(2,1)S(1)}, u32[]{:S(2)}, u32[]{:S(2)}) collective-permute-start(bf16[512,259]{0,1:T(8,128)(2,1)S(1)} %get-tuple-element.75), channel_id=1, source_target_pairs={{2,0},{3,1},{4,2},{5,3},{6,4},{7,5},{10,8},{11,9},{12,10},{13,11},... | collective-permute-start | bytes 795656 | tf_op jit(solution)/shard_map/ppermute | solution.py:13
  166.2 17.3 %copy-start.13 = (bf16[512,512]{0,1:T(8,128)(2,1)}, bf16[512,512]{0,1:T(8,128)(2,1)S(1)}, u32[]{:S(2)}) copy-start(bf16[512,512]{0,1:T(8,128)(2,1)S(1)} %get-tuple-element.87) | copy-start | bytes 1572868
  196.9 42.6 %collective-permute-start.6 = (f32[512,512]{0,1:T(8,128)}, f32[512,512]{0,1:T(8,128)S(1)}, u32[]{:S(2)}, u32[]{:S(2)}) collective-permute-start(f32[512,512]{0,1:T(8,128)} %get-tuple-element.30), channel_id=1, source_target_pairs={{1,0},{2,1},{3,2},{4,3},{5,4},{6,5},{7,6},{9,8},{10,9},{11,10},{12... | collective-permute-start | bytes 3145736 | tf_op jit(solution)/shard_map/ppermute | solution.py:13
  198.2 41.3 %collective-permute-start.7 = (f32[512,512]{0,1:T(8,128)}, f32[512,512]{0,1:T(8,128)}, u32[]{:S(2)}, u32[]{:S(2)}) collective-permute-start(f32[512,512]{0,1:T(8,128)} %get-tuple-element.31), channel_id=1, source_target_pairs={{0,1},{1,2},{2,3},{3,4},{4,5},{5,6},{6,7},{8,9},{9,10},{10,11},{11... | collective-permute-start | bytes 3145736 | tf_op jit(solution)/shard_map/ppermute | solution.py:13
  204.7 148.2 %reduce-scatter.9.cloned.1.call-start = ((), (), s32[]{:S(2)}) async-start(), calls=%async_computation.9 | async-start | bytes 2228224 | tf_op jit(solution)/shard_map/reduce_scatter | solution.py:150
  206.0 33.5 %collective-permute-start.8 = (f32[512,259]{0,1:T(8,128)S(1)}, f32[512,259]{0,1:T(8,128)S(1)}, u32[]{:S(2)}, u32[]{:S(2)}) collective-permute-start(f32[512,259]{0,1:T(8,128)S(1)} %get-tuple-element.32), channel_id=1, source_target_pairs={{2,0},{3,1},{4,2},{5,3},{6,4},{7,5},{10,8},{11,9},{12,10},{13,11},... | collective-permute-start | bytes 1591304 | tf_op jit(solution)/shard_map/ppermute | solution.py:13
  207.3 35.9 %copy-start.9 = (bf16[512,512]{0,1:T(8,128)(2,1)S(1)}, bf16[512,512]{0,1:T(8,128)(2,1)}, u32[]{:S(2)}) copy-start(bf16[512,512]{0,1:T(8,128)(2,1)} %copy-done.8) | copy-start | bytes 1572868
  207.3 32.2 %collective-permute-start.9 = (f32[512,259]{0,1:T(8,128)S(1)}, f32[512,259]{0,1:T(8,128)S(1)}, u32[]{:S(2)}, u32[]{:S(2)}) collective-permute-start(f32[512,259]{0,1:T(8,128)S(1)} %get-tuple-element.33), channel_id=1, source_target_pairs={{0,2},{1,3},{2,4},{3,5},{4,6},{5,7},{8,10},{9,11},{10,12},{11,13},... | collective-permute-start | bytes 1591304 | tf_op jit(solution)/shard_map/ppermute | solution.py:13
  245.3 201.4 %reduce-scatter.7.cloned.1.call-start = ((), (), s32[]{:S(2)}) async-start(), calls=%async_computation.8 | async-start | bytes 6684672 | tf_op jit(solution)/shard_map/reduce_scatter | solution.py:150
  251.1 288.5 %reduce-scatter.5.cloned.1.call-start = ((), (), s32[]{:S(2)}) async-start(), calls=%async_computation.7 | async-start | bytes 6684672 | tf_op jit(solution)/shard_map/reduce_scatter | solution.py:150
  260.7 387.5 %all-reduce.27.cloned.1.call-start = ((), (), s32[]{:S(2)}) async-start(), calls=%async_computation.11 | async-start | bytes 1966080 | tf_op jit(solution)/shard_map/psum | solution.py:149
  267.7 278.7 %copy-start.17 = (bf16[512,512]{0,1:T(8,128)(2,1)S(1)}, bf16[512,512]{0,1:T(8,128)(2,1)}, u32[]{:S(2)}) copy-start(bf16[512,512]{0,1:T(8,128)(2,1)} %copy-done.16) | copy-start | bytes 1572868
  539.7 8.2 %collective-permute-start.10 = (f32[512,131]{0,1:T(8,128)S(1)}, f32[512,131]{0,1:T(8,128)S(1)}, u32[]{:S(2)}, u32[]{:S(2)}) collective-permute-start(f32[512,131]{0,1:T(8,128)S(1)} %get-tuple-element.70), channel_id=1, source_target_pairs={{1,0},{2,1},{3,2},{4,3},{5,4},{6,5},{7,6},{9,8},{10,9},{11,10},{12... | collective-permute-start | bytes 804872 | tf_op jit(solution)/shard_map/ppermute | solution.py:13
  541.2 7.5 %collective-permute-start.11 = (f32[512,131]{0,1:T(8,128)S(1)}, f32[512,131]{0,1:T(8,128)S(1)}, u32[]{:S(2)}, u32[]{:S(2)}) collective-permute-start(f32[512,131]{0,1:T(8,128)S(1)} %get-tuple-element.71), channel_id=1, source_target_pairs={{0,1},{1,2},{2,3},{3,4},{4,5},{5,6},{6,7},{8,9},{9,10},{10,11},{11... | collective-permute-start | bytes 804872 | tf_op jit(solution)/shard_map/ppermute | solution.py:13
  548.6 104.6 %copy-start.1 = (f32[6,512]{1,0:T(8,128)S(1)}, f32[6,512]{1,0:T(8,128)}, u32[]{:S(2)}) copy-start(f32[6,512]{1,0:T(8,128)} %param.18) | copy-start | bytes 36868
  (24 other events, 80.7 us)
Sparse Core Ops, SparseCore 0:
  11.0 56.4 all-gather.7
  69.9 43.6 all-gather.5
  116.0 63.5 all-gather.9
  204.8 73.8 reduce-scatter.10
  282.9 69.9 reduce-scatter.8
  357.5 89.2 reduce-scatter.6
  451.4 88.1 reduce-scatter.4
  542.6 72.0 all-reduce.26
